TPU v7x, 32 devices: a whole 2x2x4 slice. The times are simulated.
32 devices in a mesh: dp: 8 (over z, x), seq: 4 (over y, core).
Axes of the slice: x: 2, y: 2, z: 4, core: 2. Of those that a mesh axis runs over, the one named last changes fastest.
Arguments:
- tokens: float32 [16, 256, 1024], P('dp', 'seq'), may hold values from -6 to 6
- output_cotangent: float32 [16, 256, 1024], P('dp', 'seq'), may hold values from -0.5 to 0.5
- placement: int32 [8], replicated, may hold values from 0 to 15, as said below
- inward: float32 [1024, 3072], P(('dp', 'seq'))
- outward: float32 [1024, 1024], P(('dp', 'seq')), may hold values from -0.75 to 0.75
- attend_vectors: float32 [5, 1024], P(None, ('dp', 'seq'))
- expand: float32 [1024, 4096], P(('dp', 'seq')), may hold values from -0.1875 to 0.1875
- shrink: float32 [4096, 1024], P(('dp', 'seq')), may hold values from -0.09375 to 0.09375
- feed_vectors: float32 [3, 1024], P(None, ('dp', 'seq'))
- expand_bias: float32 [4096], P(('dp', 'seq')), may hold values from -3 to 3
- inward_moments: float32 [2, 1024, 3072], P(None, ('dp', 'seq')), as said below
- outward_moments: float32 [2, 1024, 1024], P(None, ('dp', 'seq'))
- attend_moments: float32 [2, 5, 1024], P(None, None, ('dp', 'seq'))
- expand_moments: float32 [2, 1024, 4096], P(None, ('dp', 'seq'))
- shrink_moments: float32 [2, 4096, 1024], P(None, ('dp', 'seq'))
- feed_moments: float32 [2, 3, 1024], P(None, None, ('dp', 'seq'))
- bias_moments: float32 [2, 4096], P(None, ('dp', 'seq'))
Outputs:
- block_output: float32 [16, 256, 1024], P('dp', 'seq')
- input_gradient: float32 [16, 256, 1024], P('dp', 'seq')
- inward_gradient: float32 [1024, 3072], P(('dp', 'seq'))
- outward_gradient: float32 [1024, 1024], P(('dp', 'seq'))
- attend_gradient: float32 [5, 1024], P(None, ('dp', 'seq'))
- expand_gradient: float32 [1024, 4096], P(('dp', 'seq'))
- shrink_gradient: float32 [4096, 1024], P(('dp', 'seq'))
- feed_gradient: float32 [3, 1024], P(None, ('dp', 'seq'))
- bias_gradient: float32 [4096], P(('dp', 'seq'))
- inward_new: float32 [1024, 3072], P(('dp', 'seq'))
- outward_new: float32 [1024, 1024], P(('dp', 'seq'))
- attend_new: float32 [5, 1024], P(None, ('dp', 'seq'))
- expand_new: float32 [1024, 4096], P(('dp', 'seq'))
- shrink_new: float32 [4096, 1024], P(('dp', 'seq'))
- feed_new: float32 [3, 1024], P(None, ('dp', 'seq'))
- bias_new: float32 [4096], P(('dp', 'seq'))
- inward_state: float32 [2, 1024, 3072], P(None, ('dp', 'seq'))
- outward_state: float32 [2, 1024, 1024], P(None, ('dp', 'seq'))
- attend_state: float32 [2, 5, 1024], P(None, None, ('dp', 'seq'))
- expand_state: float32 [2, 1024, 4096], P(None, ('dp', 'seq'))
- shrink_state: float32 [2, 4096, 1024], P(None, ('dp', 'seq'))
- feed_state: float32 [2, 3, 1024], P(None, None, ('dp', 'seq'))
- bias_state: float32 [2, 4096], P(None, ('dp', 'seq'))
Inputs may be any that keep to these rules, and one draw needn't show every extreme that they name: `placement`: entries are distinct slot numbers; slot s belongs to index s // 2 of dp; in every draw some index of dp holds 2 sequences. `inward_moments`: the second moment (index 1) is positive.
All inputs are finite; a program needn't handle non-finite values.
Results may differ from a plain program's by a relative error of at most 0.012.
Values may be sent and summed in bfloat16 or wider, within the bound.
A program may use at most 192 MiB of HBM per device.

v0:
```python
import math
import jax
import jax.numpy as jnp
from jax import lax
from jax.sharding import PartitionSpec as P

HEADS = 16
HEAD_DIM = 64
norm_epsilon = 1e-05
beta_first = 0.9
beta_second = 0.95
adam_epsilon = 1e-08
learn_rate = 0.01
weight_decay = 0.1
adam_steps = 4
gelu_scale = 0.7978845608028654
gelu_cubic = 0.044715
masked_score = -1e30


def halved(operand):
    return operand.astype(jnp.bfloat16)


def normalize(operand):
    average = jnp.mean(operand, axis=-1, keepdims=True)
    centered = operand - average
    variance = jnp.mean(centered * centered, axis=-1, keepdims=True)
    inverse = lax.rsqrt(variance + norm_epsilon)
    return (centered * inverse, inverse)


def norm_back(upstream, normed, inverse):
    first_mean = jnp.mean(upstream, axis=-1, keepdims=True)
    second_mean = jnp.mean(upstream * normed, axis=-1, keepdims=True)
    return inverse * (upstream - first_mean - normed * second_mean)


def gelu_pair(upper):
    inner_arg = gelu_scale * (upper + gelu_cubic * upper * upper * upper)
    tangent = jnp.tanh(inner_arg)
    active = 0.5 * upper * (1.0 + tangent)
    slope = 0.5 * (1.0 + tangent) + 0.5 * upper * (1.0 - tangent * tangent) * gelu_scale * (
        1.0 + 3.0 * gelu_cubic * upper * upper
    )
    return (active, slope)


def adamw_update(parameter, gradient, moments, decay_rate):
    first_moment = beta_first * moments[0] + (1.0 - beta_first) * gradient
    second = beta_second * moments[1] + (1.0 - beta_second) * gradient * gradient
    unbiased_first = first_moment / (1.0 - beta_first**adam_steps)
    unbiased_second = second / (1.0 - beta_second**adam_steps)
    update = unbiased_first / (jnp.sqrt(unbiased_second) + adam_epsilon) + decay_rate * parameter
    return (parameter - learn_rate * update, jnp.stack([first_moment, second]))


def spread_columns(piece, groups, inner):
    rows = piece.shape[0]
    parts = piece.reshape(rows, -1, groups, inner)
    moved = lax.all_to_all(parts, "seq", 2, 0, tiled=True)
    return moved.reshape(groups * rows, -1)


def collect_columns(piece, groups, inner):
    rows = piece.shape[0] // groups
    parts = piece.reshape(rows * groups, -1, 1, inner)
    moved = lax.all_to_all(parts, "seq", 0, 2, tiled=True)
    return moved.reshape(rows, -1)


def body(
    tokens,
    output_cotangent,
    placement,
    inward,
    outward,
    attend_vectors,
    expand,
    shrink,
    feed_vectors,
    expand_bias,
    inward_moments,
    outward_moments,
    attend_moments,
    expand_moments,
    shrink_moments,
    feed_moments,
    bias_moments,
):
    slot_count, block_size, model_width = tokens.shape
    groups = lax.axis_size("seq")
    replicas = lax.axis_size("dp")
    devices = groups * replicas
    mine = lax.axis_index("seq")
    length = block_size * groups
    row_count = slot_count * block_size
    all_rows = slot_count * length
    head_count = HEADS // groups
    part_width = head_count * HEAD_DIM
    vec_width = attend_vectors.shape[1]
    hidden_part = expand_bias.shape[0]
    score_scale = 1.0 / math.sqrt(HEAD_DIM)
    whole = ("dp", "seq")

    def gather_rows(local):
        full = lax.all_gather(local.reshape(slot_count, block_size, -1), "seq", axis=1, tiled=True)
        return full.reshape(all_rows, -1)

    def scatter_rows(partial):
        own = lax.psum_scatter(
            halved(partial).reshape(slot_count, length, -1), "seq", scatter_dimension=1, tiled=True
        )
        return own.reshape(row_count, -1).astype(jnp.float32)

    slot_ids = lax.axis_index("dp") * slot_count + jnp.arange(slot_count, dtype=jnp.int32)
    live_mask = jnp.any(placement[None, :] == slot_ids[:, None], axis=1).astype(jnp.float32)[
        :, None, None
    ]
    small = jnp.concatenate(
        [halved(attend_vectors).reshape(-1), halved(feed_vectors).reshape(-1), halved(expand_bias)]
    )
    small_rows = 16
    small_block = jnp.pad(small, (0, small_rows * model_width - small.shape[0])).reshape(
        small_rows, model_width
    )
    out_rows = outward.shape[0]
    first = lax.all_gather(
        jnp.concatenate([halved(outward), small_block], axis=0), whole, axis=0, tiled=True
    ).reshape(devices, out_rows + small_rows, model_width)
    out_whole = first[:, :out_rows].reshape(devices * out_rows, model_width)
    small_all = first[:, out_rows:].reshape(devices, -1)[:, : small.shape[0]].astype(jnp.float32)
    vectors = jnp.transpose(
        small_all[:, : 8 * vec_width].reshape(devices, 8, vec_width), (1, 0, 2)
    ).reshape(8, model_width)
    vec_one = vectors[:5]
    vec_two = vectors[5:]
    bias_all = small_all[:, 8 * vec_width :].reshape(replicas, groups, hidden_part)
    bias_part = lax.dynamic_index_in_dim(bias_all, mine, 1, keepdims=False).reshape(-1)
    in_width = 3 * part_width
    moved_in = spread_columns(halved(inward), groups, part_width)
    moved_up = spread_columns(halved(expand), groups, hidden_part)
    in_part = lax.all_gather(moved_in, "dp", axis=0, tiled=True)
    up_part = lax.all_gather(moved_up, "dp", axis=0, tiled=True)
    down_part = lax.all_gather(halved(shrink), "dp", axis=0, tiled=True)
    cotangent = (output_cotangent * live_mask).reshape(row_count, model_width)
    cot_all = gather_rows(halved(cotangent))
    feed_bias_grad = jnp.sum(cotangent, axis=0)
    flat_tokens = tokens.reshape(row_count, model_width)
    normed_one, inverse_one = normalize(flat_tokens)
    lifted_one = gather_rows(halved(normed_one * vec_one[0] + vec_one[1]))
    packed = jnp.dot(lifted_one, in_part, preferred_element_type=jnp.float32)
    bias_query = lax.dynamic_slice_in_dim(vec_one[2], mine * part_width, part_width)
    bias_value = lax.dynamic_slice_in_dim(vec_one[3], mine * part_width, part_width)

    def to_heads(operand):
        return jnp.transpose(
            operand.reshape(slot_count, length, head_count, HEAD_DIM), (0, 2, 1, 3)
        )

    def from_heads(operand):
        return jnp.transpose(operand, (0, 2, 1, 3)).reshape(all_rows, part_width)

    queries = to_heads(halved(packed[:, :part_width] + bias_query))
    keys = to_heads(halved(packed[:, part_width : 2 * part_width]))
    values = to_heads(halved(packed[:, 2 * part_width :] + bias_value))
    positions = jnp.arange(length)
    allowed = positions[None, :] <= positions[:, None]
    scores = (
        jnp.einsum("shqd,shkd->shqk", queries, keys, preferred_element_type=jnp.float32)
        * score_scale
    )
    scores = jnp.where(allowed, scores, masked_score)
    score_peak = jnp.max(scores, axis=-1, keepdims=True)
    log_total = score_peak + jnp.log(jnp.sum(jnp.exp(scores - score_peak), axis=-1, keepdims=True))
    weights_full = jnp.exp(scores - log_total)
    weights_half = halved(weights_full)
    attended_heads = halved(
        jnp.einsum("shqk,shkd->shqd", weights_half, values, preferred_element_type=jnp.float32)
    )
    attended = lax.all_to_all(
        from_heads(attended_heads).reshape(slot_count, length, part_width), "seq", 1, 2, tiled=True
    ).reshape(row_count, model_width)
    projected = jnp.dot(attended, out_whole, preferred_element_type=jnp.float32)
    middle = flat_tokens + projected + vec_one[4]
    normed_two, inverse_two = normalize(middle)
    lifted_two = gather_rows(halved(normed_two * vec_two[0] + vec_two[1]))
    upper = jnp.dot(lifted_two, up_part, preferred_element_type=jnp.float32) + bias_part
    active_full, slope = gelu_pair(upper)
    active = halved(active_full)
    upper_grad = (
        lax.dot_general(
            cot_all, down_part, (((1,), (1,)), ((), ())), preferred_element_type=jnp.float32
        )
        * slope
    )
    upper_half = halved(upper_grad)
    lift_two_grad = scatter_rows(
        lax.dot_general(
            upper_half, up_part, (((1,), (1,)), ((), ())), preferred_element_type=jnp.float32
        )
    )
    fed = scatter_rows(jnp.dot(active, down_part, preferred_element_type=jnp.float32))
    block_output = (middle + fed + vec_two[2]).reshape(
        slot_count, block_size, model_width
    ) * live_mask

    def outer(left, right):
        return halved(
            lax.dot_general(
                left, right, (((0,), (0,)), ((), ())), preferred_element_type=jnp.float32
            )
        )

    shrink_sum = lax.psum_scatter(
        outer(active, cot_all), "dp", scatter_dimension=0, tiled=True
    ).astype(jnp.float32)
    expand_sum = collect_columns(
        lax.psum_scatter(outer(lifted_two, upper_half), "dp", scatter_dimension=0, tiled=True),
        groups,
        hidden_part,
    ).astype(jnp.float32)
    bias_grad = jnp.sum(upper_grad, axis=0).reshape(replicas, 1, hidden_part)
    gain_two_grad = jnp.sum(lift_two_grad * normed_two, axis=0)
    shift_two_grad = jnp.sum(lift_two_grad, axis=0)
    middle_grad = cotangent + norm_back(lift_two_grad * vec_two[0], normed_two, inverse_two)
    middle_half = halved(middle_grad)
    out_bias_grad = jnp.sum(middle_grad, axis=0)
    attended_back = halved(
        lax.dot_general(
            middle_half, out_whole, (((1,), (1,)), ((), ())), preferred_element_type=jnp.float32
        )
    )
    attended_grad = to_heads(
        lax.all_to_all(
            attended_back.reshape(slot_count, block_size, model_width), "seq", 2, 1, tiled=True
        ).reshape(all_rows, part_width)
    )
    outward_sum = lax.psum_scatter(
        outer(attended, middle_half), whole, scatter_dimension=0, tiled=True
    ).astype(jnp.float32)
    delta_sum = jnp.sum(
        attended_grad.astype(jnp.float32) * attended_heads.astype(jnp.float32),
        axis=-1,
        keepdims=True,
    )
    weight_grad = jnp.einsum(
        "shqd,shkd->shqk", attended_grad, values, preferred_element_type=jnp.float32
    )
    score_grad = halved(weights_full * (weight_grad - delta_sum) * score_scale)
    query_grad = from_heads(
        jnp.einsum("shqk,shkd->shqd", score_grad, keys, preferred_element_type=jnp.float32)
    )
    key_grad = from_heads(
        jnp.einsum("shqk,shqd->shkd", score_grad, queries, preferred_element_type=jnp.float32)
    )
    value_grad = from_heads(
        jnp.einsum(
            "shqk,shqd->shkd", weights_half, attended_grad, preferred_element_type=jnp.float32
        )
    )
    packed_grad = halved(jnp.concatenate([query_grad, key_grad, value_grad], axis=1))
    lift_one_grad = scatter_rows(
        lax.dot_general(
            packed_grad, in_part, (((1,), (1,)), ((), ())), preferred_element_type=jnp.float32
        )
    )
    inward_sum = collect_columns(
        lax.psum_scatter(outer(lifted_one, packed_grad), "dp", scatter_dimension=0, tiled=True),
        groups,
        part_width,
    ).astype(jnp.float32)

    def place_part(part):
        return lax.dynamic_update_slice_in_dim(
            jnp.zeros((model_width,), jnp.float32), part, mine * part_width, 0
        )

    gain_one_grad = jnp.sum(lift_one_grad * normed_one, axis=0)
    shift_one_grad = jnp.sum(lift_one_grad, axis=0)
    tokens_grad = middle_grad + norm_back(lift_one_grad * vec_one[0], normed_one, inverse_one)
    input_gradient = tokens_grad.reshape(slot_count, block_size, model_width) * live_mask
    vector_grads = jnp.stack(
        [
            gain_one_grad,
            shift_one_grad,
            place_part(jnp.sum(query_grad, axis=0)),
            place_part(jnp.sum(value_grad, axis=0)),
            out_bias_grad,
            gain_two_grad,
            shift_two_grad,
            feed_bias_grad,
        ]
    ).T
    bias_placed = lax.dynamic_update_slice_in_dim(
        jnp.zeros((replicas, groups, hidden_part), jnp.float32), bias_grad, mine, 1
    ).reshape(model_width, -1)
    small_sum = lax.psum_scatter(
        jnp.concatenate([vector_grads, bias_placed], axis=1), whole, scatter_dimension=0, tiled=True
    )
    attend_vec_sum = small_sum[:, :5].T
    feed_vec_sum = small_sum[:, 5:8].T
    bias_sum = small_sum[:, 8:].reshape(-1)
    inward_new, inward_state = adamw_update(inward, inward_sum, inward_moments, weight_decay)
    outward_new, outward_state = adamw_update(outward, outward_sum, outward_moments, weight_decay)
    attend_new, attend_state = adamw_update(attend_vectors, attend_vec_sum, attend_moments, 0.0)
    expand_new, expand_state = adamw_update(expand, expand_sum, expand_moments, weight_decay)
    shrink_new, shrink_state = adamw_update(shrink, shrink_sum, shrink_moments, weight_decay)
    feed_new, feed_state = adamw_update(feed_vectors, feed_vec_sum, feed_moments, 0.0)
    bias_new, bias_state = adamw_update(expand_bias, bias_sum, bias_moments, 0.0)
    return (
        block_output,
        input_gradient,
        inward_sum,
        outward_sum,
        attend_vec_sum,
        expand_sum,
        shrink_sum,
        feed_vec_sum,
        bias_sum,
        inward_new,
        outward_new,
        attend_new,
        expand_new,
        shrink_new,
        feed_new,
        bias_new,
        inward_state,
        outward_state,
        attend_state,
        expand_state,
        shrink_state,
        feed_state,
        bias_state,
    )


def solution(mesh):
    placed = (
        P("dp", "seq", None),
        P("dp", "seq", None),
        P(),
        P(("dp", "seq"), None),
        P(("dp", "seq"), None),
        P(None, ("dp", "seq")),
        P(("dp", "seq"), None),
        P(("dp", "seq"), None),
        P(None, ("dp", "seq")),
        P(("dp", "seq")),
        P(None, ("dp", "seq"), None),
        P(None, ("dp", "seq"), None),
        P(None, None, ("dp", "seq")),
        P(None, ("dp", "seq"), None),
        P(None, ("dp", "seq"), None),
        P(None, None, ("dp", "seq")),
        P(None, ("dp", "seq")),
    )
    return jax.shard_map(
        body,
        mesh=mesh,
        in_specs=placed,
        out_specs=(
            P("dp", "seq", None),
            P("dp", "seq", None),
            P(("dp", "seq"), None),
            P(("dp", "seq"), None),
            P(None, ("dp", "seq")),
            P(("dp", "seq"), None),
            P(("dp", "seq"), None),
            P(None, ("dp", "seq")),
            P(("dp", "seq")),
            P(("dp", "seq"), None),
            P(("dp", "seq"), None),
            P(None, ("dp", "seq")),
            P(("dp", "seq"), None),
            P(("dp", "seq"), None),
            P(None, ("dp", "seq")),
            P(("dp", "seq")),
            P(None, ("dp", "seq"), None),
            P(None, ("dp", "seq"), None),
            P(None, None, ("dp", "seq")),
            P(None, ("dp", "seq"), None),
            P(None, ("dp", "seq"), None),
            P(None, None, ("dp", "seq")),
            P(None, ("dp", "seq")),
        ),
        check_vma=False,
    )
```

profile of v0, /device:TPU:0, one launch (start us, length us, event | category | flops | bytes accessed | tf_op | source)
XLA Modules:
  0.0 881.6 jit_solution(11967319726546057766)
XLA Ops:
  12.4 9.4 %all_to_all.78 = bf16[32,3,4,256]{3,0,1,2:T(8,128)(2,1)S(1)} all-to-all(bf16[32,3,4,256]{3,0,1,2:T(8,128)(2,1)S(1)} %copy.236), channel_id=1, replica_groups=mesh['dp'=8,'seq'=4] {'seq'}, dimensions={2} | all-to-all | bytes 393216 | tf_op jit(solution)/shard_map/all_to_all | solution.py:61
  23.1 50.3 %all-gather.8.cloned.1.call-done = bf16[1536,1024]{1,0:T(8,128)(2,1)} async-done(((bf16[48,1024]{1,0:T(8,128)(2,1)}), bf16[1536,1024]{1,0:T(8,128)(2,1)}) %all-gather.8.cloned.1.call-update) | async-done | bytes 3145744 | tf_op jit(solution)/shard_map/all_gather | solution.py:128
  73.4 1.3 slice.155
  77.6 8.5 all_to_all.79
  87.3 31.8 %all-gather.12.cloned.1.call-done = bf16[1024,768]{1,0:T(8,128)(2,1)} async-done(((bf16[128,768]{1,0:T(8,128)(2,1)}), bf16[1024,768]{1,0:T(8,128)(2,1)}) %all-gather.12.cloned.1.call-update) | async-done | bytes 1572880 | tf_op jit(solution)/shard_map/all_gather | solution.py:143
  119.1 17.2 %all-gather.10.cloned.1.call-done = bf16[2,256,1024]{2,1,0:T(8,128)(2,1)} async-done(((bf16[2,64,1024]{2,1,0:T(8,128)(2,1)}), bf16[2,256,1024]{2,1,0:T(8,128)(2,1)}) %all-gather.10.cloned.1.call-update) | async-done | bytes 1048592 | tf_op jit(solution)/shard_map/all_gather | solution.py:107
  136.3 2.7 fusion.89
  142.3 3.4 all-to-all-start.1
  145.8 3.3 slice.165
  149.4 2.3 all-to-all-done.1
  152.0 2.2 fusion.87
  158.5 29.5 %all-gather.16.cloned.1.call-done = bf16[1024,1024]{1,0:T(8,128)(2,1)} async-done(((bf16[128,1024]{1,0:T(8,128)(2,1)}), bf16[1024,1024]{1,0:T(8,128)(2,1)}) %all-gather.16.cloned.1.call-update) | async-done | bytes 2097168 | tf_op jit(solution)/shard_map/all_gather | solution.py:144
  188.0 17.3 %all-gather.14.cloned.1.call-done = bf16[2,256,1024]{2,1,0:T(8,128)(2,1)} async-done(((bf16[2,64,1024]{2,1,0:T(8,128)(2,1)}), bf16[2,256,1024]{2,1,0:T(8,128)(2,1)}) %all-gather.14.cloned.1.call-update) | async-done | bytes 1048592 | tf_op jit(solution)/shard_map/all_gather | solution.py:107
  205.3 4.5 fusion.90
  209.8 14.2 %all-gather.20.cloned.1.call-done = bf16[2,256,1024]{2,1,0:T(8,128)(2,1)} async-done(((bf16[2,64,1024]{2,1,0:T(8,128)(2,1)}), bf16[2,256,1024]{2,1,0:T(8,128)(2,1)}) %all-gather.20.cloned.1.call-update) | async-done | bytes 1048592 | tf_op jit(solution)/shard_map/all_gather | solution.py:107
  224.0 4.9 convolution_convert_fusion
  229.0 68.5 %reduce-scatter.23.cloned.1.call-done = bf16[128,1024]{1,0:T(8,128)(2,1)} async-done(((bf16[1024,1024]{1,0:T(8,128)(2,1)}), bf16[128,1024]{1,0:T(8,128)(2,1)}) %reduce-scatter.23.cloned.1.call-update) | async-done | bytes 262160 | tf_op jit(solution)/shard_map/reduce_scatter | solution.py:215
  297.5 2.1 fusion.55
  299.6 1.5 fusion.59
  301.4 48.0 %all-gather.18.cloned.1.call-done = bf16[1024,1024]{1,0:T(8,128)(2,1)} async-done(((bf16[128,1024]{1,0:T(8,128)(2,1)}), bf16[1024,1024]{1,0:T(8,128)(2,1)}) %all-gather.18.cloned.1.call-update) | async-done | bytes 2097168 | tf_op jit(solution)/shard_map/all_gather | solution.py:145
  349.4 5.1 fusion.88
  354.5 2.3 convolution_convert_fusion.5
  356.9 4.7 convolution_convert_fusion.6
  361.7 18.6 %reduce-scatter.13.cloned.1.call-done = bf16[2,64,1024]{2,1,0:T(8,128)(2,1)} async-done(((bf16[2,256,1024]{2,1,0:T(8,128)(2,1)}), bf16[2,64,1024]{2,1,0:T(8,128)(2,1)}) %reduce-scatter.13.cloned.1.call-update) | async-done | bytes 262160 | tf_op jit(solution)/shard_map/reduce_scatter | solution.py:111
  381.5 1.2 fusion.32
  382.7 25.3 %reduce-scatter.11.cloned.1.call-done = bf16[2,64,1024]{2,1,0:T(8,128)(2,1)} async-done(((bf16[2,256,1024]{2,1,0:T(8,128)(2,1)}), bf16[2,64,1024]{2,1,0:T(8,128)(2,1)}) %reduce-scatter.11.cloned.1.call-update) | async-done | bytes 262160 | tf_op jit(solution)/shard_map/reduce_scatter | solution.py:111
  408.0 2.4 fusion.81
  412.3 1.5 reshape.573
  413.8 9.1 %all_to_all.80 = bf16[4,2,16384]{2,1,0:T(2,128)(2,1)} all-to-all(bf16[4,2,16384]{2,1,0:T(2,128)(2,1)S(1)} %reshape.573), channel_id=1, replica_groups=mesh['dp'=8,'seq'=4] {'seq'}, dimensions={0} | all-to-all | bytes 524288 | tf_op jit(solution)/shard_map/all_to_all | solution.py:235
  422.9 2.1 reshape.574
  425.0 2.2 copy.345
  427.3 1.5 reshape.528
  432.7 2.0 convolution_convert_fusion.4
  435.1 2.6 convolution_convert_fusion.1
  438.8 21.0 %reduce-scatter.15.cloned.1.call-done = bf16[2,64,1024]{2,1,0:T(8,128)(2,1)} async-done(((bf16[2,256,1024]{2,1,0:T(8,128)(2,1)}), bf16[2,64,1024]{2,1,0:T(8,128)(2,1)}) %reduce-scatter.15.cloned.1.call-update) | async-done | bytes 262160 | tf_op jit(solution)/shard_map/reduce_scatter | solution.py:111
  459.7 1.2 multiply_reduce_fusion
  462.2 3.5 convolution_convert_fusion.3
  467.1 2.1 convolution_convert_fusion.2
  469.2 62.3 %reduce-scatter.21.cloned.1.call-done = bf16[128,1024]{1,0:T(8,128)(2,1)} async-done(((bf16[1024,1024]{1,0:T(8,128)(2,1)}), bf16[128,1024]{1,0:T(8,128)(2,1)}) %reduce-scatter.21.cloned.1.call-update) | async-done | bytes 262160 | tf_op jit(solution)/shard_map/reduce_scatter | solution.py:219
  531.4 1.7 copy.304
  533.1 3.4 all-to-all-start.5
  538.1 4.5 all-to-all-done.5
  544.7 1.2 multiply_subtract_fusion.1
  545.9 122.6 %reduce-scatter.25.cloned.1.call-done = f32[32,12]{1,0:T(8,128)} async-done(((f32[1024,12]{1,0:T(8,128)}), f32[32,12]{1,0:T(8,128)}) %reduce-scatter.25.cloned.1.call-update) | async-done | bytes 1552
  673.0 60.3 %reduce-scatter.17.cloned.1.call-done = bf16[128,768]{1,0:T(8,128)(2,1)} async-done(((bf16[1024,768]{1,0:T(8,128)(2,1)}), bf16[128,768]{1,0:T(8,128)(2,1)}) %reduce-scatter.17.cloned.1.call-update) | async-done | bytes 196624 | tf_op jit(solution)/shard_map/reduce_scatter | solution.py:269
  735.3 3.5 all-to-all-start.4
  740.6 4.9 all-to-all-done.4
  748.5 124.2 %reduce-scatter.19.cloned.1.call-done = bf16[32,1024]{1,0:T(8,128)(2,1)} async-done(((bf16[1024,1024]{1,0:T(8,128)(2,1)}), bf16[32,1024]{1,0:T(8,128)(2,1)}) %reduce-scatter.19.cloned.1.call-update) | async-done | bytes 65552 | tf_op jit(solution)/shard_map/reduce_scatter | solution.py:239
  (273 shorter events, 46.6 us)
Async XLA Ops:
  7.2 15.6 %copy-start.1 = (f32[2,64,1024]{2,1,0:T(8,128)S(1)}, f32[2,64,1024]{2,1,0:T(8,128)}, u32[]{:S(2)}) copy-start(f32[2,64,1024]{2,1,0:T(8,128)} %param.17) | copy-start | bytes 1572868
  7.2 66.2 %all-gather.8.cloned.1.call-start = ((), (), s32[]{:S(2)}) async-start(), calls=%async_computation.14 | async-start | bytes 3244032 | tf_op jit(solution)/shard_map/all_gather | solution.py:128
  11.2 107.9 %all-gather.12.cloned.1.call-start = ((), (), s32[]{:S(2)}) async-start(), calls=%async_computation.16 | async-start | bytes 1769472 | tf_op jit(solution)/shard_map/all_gather | solution.py:143
  22.7 113.6 %all-gather.10.cloned.1.call-start = ((), (), s32[]{:S(2)}) async-start(), calls=%async_computation.15 | async-start | bytes 1310720 | tf_op jit(solution)/shard_map/all_gather | solution.py:107
  74.7 2.7 copy-start.16
  77.3 110.7 %all-gather.16.cloned.1.call-start = ((), (), s32[]{:S(2)}) async-start(), calls=%async_computation.18 | async-start | bytes 2359296 | tf_op jit(solution)/shard_map/all_gather | solution.py:144
  141.5 7.7 copy-start.8
  142.3 9.4 %all-to-all-start.1 = ((bf16[2,256,256]{2,0,1:T(2,128)(2,1)}), bf16[2,256,256]{2,0,1:T(2,128)(2,1)S(1)}, u32[]{:S(2)}, u32[]{:S(2)}) async-start(bf16[2,256,256]{2,0,1:T(2,128)(2,1)} %copy.245), calls=%async_computation.1 | async-start | bytes 524288 | tf_op jit(solution)/shard_map/all_to_all | solution.py:181
  145.8 3.4 copy-start.34
  145.8 3.5 copy-start.33
  145.8 3.5 copy-start.32
  145.8 59.5 %all-gather.14.cloned.1.call-start = ((), (), s32[]{:S(2)}) async-start(), calls=%async_computation.17 | async-start | bytes 1310720 | tf_op jit(solution)/shard_map/all_gather | solution.py:107
  152.0 3.4 copy-start.10
  152.0 3.4 copy-start.47
  155.4 68.6 %all-gather.20.cloned.1.call-start = ((), (), s32[]{:S(2)}) async-start(), calls=%async_computation.21 | async-start | bytes 1310720 | tf_op jit(solution)/shard_map/all_gather | solution.py:107
  158.4 139.1 %reduce-scatter.23.cloned.1.call-start = ((), (), s32[]{:S(2)}) async-start(), calls=%async_computation.27 | async-start | bytes 2359296 | tf_op jit(solution)/shard_map/reduce_scatter | solution.py:215
  228.9 120.5 %all-gather.18.cloned.1.call-start = ((), (), s32[]{:S(2)}) async-start(), calls=%async_computation.19 | async-start | bytes 2359296 | tf_op jit(solution)/shard_map/all_gather | solution.py:145
  301.2 79.1 %reduce-scatter.13.cloned.1.call-start = ((), (), s32[]{:S(2)}) async-start(), calls=%async_computation.22 | async-start | bytes 1310720 | tf_op jit(solution)/shard_map/reduce_scatter | solution.py:111
  349.4 5.1 copy-start.44
  356.8 51.2 %reduce-scatter.11.cloned.1.call-start = ((), (), s32[]{:S(2)}) async-start(), calls=%async_computation.20 | async-start | bytes 1310720 | tf_op jit(solution)/shard_map/reduce_scatter | solution.py:111
  361.6 98.2 %reduce-scatter.15.cloned.1.call-start = ((), (), s32[]{:S(2)}) async-start(), calls=%async_computation.23 | async-start | bytes 1310720 | tf_op jit(solution)/shard_map/reduce_scatter | solution.py:111
  408.0 2.4 copy-start
  412.3 16.4 %copy-start.9 = (bf16[2,4,256,64]{2,3,1,0:T(8,128)(2,1)S(1)}, bf16[2,4,256,64]{2,3,1,0:T(8,128)(2,1)}, u32[]{:S(2)}) copy-start(bf16[2,4,256,64]{2,3,1,0:T(8,128)(2,1)} %copy-done.8) | copy-start | bytes 786436
  432.7 2.3 copy-start.49
  434.8 96.7 %reduce-scatter.21.cloned.1.call-start = ((), (), s32[]{:S(2)}) async-start(), calls=%async_computation.26 | async-start | bytes 2359296 | tf_op jit(solution)/shard_map/reduce_scatter | solution.py:219
  437.7 24.5 %copy-start.31 = (bf16[512,768]{0,1:T(8,128)(2,1)S(1)}, bf16[512,768]{0,1:T(8,128)(2,1)}, u32[]{:S(2)}) copy-start(bf16[512,768]{0,1:T(8,128)(2,1)} %copy-done.30) | copy-start | bytes 2359300
  437.7 230.8 %reduce-scatter.25.cloned.1.call-start = ((), (), s32[]{:S(2)}) async-start(), calls=%async_computation.28 | async-start | bytes 540672
  462.1 3.9 copy-start.41
  462.1 3.9 copy-start.39
  462.1 3.9 copy-start.20
  462.1 3.9 copy-start.22
  462.2 271.2 %reduce-scatter.17.cloned.1.call-start = ((), (), s32[]{:S(2)}) async-start(), calls=%async_computation.24 | async-start | bytes 1769472 | tf_op jit(solution)/shard_map/reduce_scatter | solution.py:269
  465.8 406.9 %reduce-scatter.19.cloned.1.call-start = ((), (), s32[]{:S(2)}) async-start(), calls=%async_computation.25 | async-start | bytes 2162688 | tf_op jit(solution)/shard_map/reduce_scatter | solution.py:239
  469.1 67.6 %copy-start.25 = (bf16[2,64,1024]{2,1,0:T(8,128)(2,1)S(1)}, bf16[2,64,1024]{2,1,0:T(8,128)(2,1)}, u32[]{:S(2)}) copy-start(bf16[2,64,1024]{2,1,0:T(8,128)(2,1)} %reduce-scatter.15.cloned.1.call-done) | copy-start | bytes 786436
  469.1 67.8 %copy-start.21 = (f32[128,1024]{1,0:T(8,128)S(1)}, f32[128,1024]{1,0:T(8,128)}, u32[]{:S(2)}) copy-start(f32[128,1024]{1,0:T(8,128)} %get-tuple-element.221) | copy-start | bytes 1572868
  533.1 9.5 %all-to-all-start.5 = ((bf16[128,8,1,128]{3,1,2,0:T(8,128)(2,1)}), bf16[128,8,1,128]{3,1,2,0:T(8,128)(2,1)S(1)}, u32[]{:S(2)}, u32[]{:S(2)}) async-start(bf16[128,8,1,128]{3,1,2,0:T(8,128)(2,1)} %bitcast.49), calls=%async_computation.11 | async-start | bytes 524288 | tf_op jit(solution)/shard_map/all_to_all | solution.py:68
  538.1 5.3 copy-start.5
  543.6 127.6 %copy-start.36 = (f32[5,32]{1,0:T(8,128)S(1)}, f32[5,32]{1,0:T(8,128)}, u32[]{:S(2)}) copy-start(f32[5,32]{1,0:T(8,128)} %param.22) | copy-start | bytes 1924
  543.7 128.2 %copy-start.40 = (f32[2,128]{1,0:T(2,128)S(1)}, f32[2,128]{1,0:T(2,128)}, u32[]{:S(2)}) copy-start(f32[2,128]{1,0:T(2,128)} %param.33) | copy-start | bytes 3076
  543.7 128.2 %copy-start.43 = (f32[128]{0:T(128)S(1)}, f32[128]{0:T(128)}, u32[]{:S(2)}) copy-start(f32[128]{0:T(128)} %param.26) | copy-start | bytes 1540
  543.7 128.8 %copy-start.38 = (f32[3,32]{1,0:T(4,128)S(1)}, f32[3,32]{1,0:T(4,128)}, u32[]{:S(2)}) copy-start(f32[3,32]{1,0:T(4,128)} %param.25) | copy-start | bytes 1156
  669.4 76.6 %copy-start.42 = (f32[128]{0:T(128)}, f32[128]{0:T(128)S(1)}, u32[]{:S(2)}) copy-start(f32[128]{0:T(128)S(1)} %reshape.514) | copy-start | bytes 1540
  670.4 76.0 %copy-start.35 = (f32[32,5]{0,1:T(8,128)}, f32[32,5]{0,1:T(8,128)S(1)}, u32[]{:S(2)}) copy-start(f32[32,5]{0,1:T(8,128)S(1)} %copy.292) | copy-start | bytes 1924
  671.2 75.1 %copy-start.37 = (f32[32,3]{0,1:T(4,128)}, f32[32,3]{0,1:T(4,128)S(1)}, u32[]{:S(2)}) copy-start(f32[32,3]{0,1:T(4,128)S(1)} %copy.293) | copy-start | bytes 1156
  735.3 11.0 %copy-start.6 = (f32[2,32,3072]{2,1,0:T(8,128)S(1)}, f32[2,32,3072]{2,1,0:T(8,128)}, u32[]{:S(2)}) copy-start(f32[2,32,3072]{2,1,0:T(8,128)} %param.27) | copy-start | bytes 2359300
  735.3 10.2 %all-to-all-start.4 = ((bf16[128,3,1,256]{3,1,2,0:T(4,128)(2,1)}), bf16[128,3,1,256]{3,1,2,0:T(4,128)(2,1)S(1)}, u32[]{:S(2)}, u32[]{:S(2)}) async-start(bf16[128,3,1,256]{3,1,2,0:T(4,128)(2,1)} %copy.263), calls=%async_computation.8 | async-start | bytes 524288 | tf_op jit(solution)/shard_map/all_to_all | solution.py:68
  746.5 126.2 %copy-start.26 = (f32[2,32,1024]{2,1,0:T(8,128)S(1)}, f32[2,32,1024]{2,1,0:T(8,128)}, u32[]{:S(2)}) copy-start(f32[2,32,1024]{2,1,0:T(8,128)} %param.28) | copy-start | bytes 786436
  746.5 127.1 %copy-start.28 = (f32[32,1024]{1,0:T(8,128)S(1)}, f32[32,1024]{1,0:T(8,128)}, u32[]{:S(2)}) copy-start(f32[32,1024]{1,0:T(8,128)} %param.21) | copy-start | bytes 393220
  (20 other events, 29.4 us)
Sparse Core Ops, SparseCore 0:
  11.5 61.8 all-gather.7
  76.2 42.8 all-gather.11
  121.2 15.0 all-gather.9
  138.9 49.0 all-gather.15
  190.0 15.2 all-gather.13
  207.3 16.6 all-gather.19
  229.1 68.4 reduce-scatter.22
  301.3 48.1 all-gather.17
  356.9 23.2 reduce-scatter.12
  383.2 24.7 reduce-scatter.10
  434.9 24.8 reduce-scatter.14
  463.1 68.2 reduce-scatter.20
  533.7 134.8 reduce-scatter.24
  671.8 61.4 reduce-scatter.16
  735.4 137.2 reduce-scatter.18
where the time goes:
time: 883 us; the launch traced here: 882 us
  waiting for transfers between devices  723 us (82%)
  matrix products  40.4 us (5%)
  local copies, waits for them, and re-layouts  33.8 us (4%)
  other arithmetic  31 us (4%)
  blocking collectives  27 us (3%)
  between operations  15 us (2%)
  starting transfers between devices  11.4 us (1%)
    reduce_scatter x1, waiting for transfers between devices, body(): lax.psum_scatter(outer(attended, middle_half), whole, scatter_dimension=0...  124 us
    unnamed x16, waiting for transfers between devices  123 us
    reduce_scatter x1, waiting for transfers between devices, body(): lax.psum_scatter(outer(active, cot_all), 'dp', scatter_dimension=0, tiled...  68.5 us
    reduce_scatter x3, waiting for transfers between devices, scatter_rows(): lax.psum_scatter(halved(partial).reshape(slot_count, length, -1), 'seq',...  64.8 us
    reduce_scatter x1, waiting for transfers between devices, body(): lax.psum_scatter(outer(lifted_two, upper_half), 'dp', scatter_dimension=0...  62.3 us
    reduce_scatter x1, waiting for transfers between devices, body(): lax.psum_scatter(outer(lifted_one, packed_grad), 'dp', scatter_dimension=...  60.3 us
    all_gather x1, waiting for transfers between devices, body(): lax.all_gather(jnp.concatenate([halved(outward), small_block], axis=0), w...  50.3 us
    all_gather x3, waiting for transfers between devices, gather_rows(): lax.all_gather(local.reshape(slot_count, block_size, -1), 'seq', axis=1,...  48.7 us
  transfers between devices with their start and end apart: 18, of which 18 were waited for; matrix products, arithmetic and copies ran while one was open for 7% of the time, Pallas kernels for 0%

commit v1 on v0

--- a/solution.py
+++ b/solution.py
@@ -16,6 +16,27 @@
 gelu_scale = 0.7978845608028654
 gelu_cubic = 0.044715
 masked_score = -1e30
+
+
+def collect(value, axis, dim):
+    size, index, extent = (lax.axis_size(axis), lax.axis_index(axis), value.shape[dim])
+    right = [(i, (i + 1) % size) for i in range(size)]
+    left = [(i, (i - 1) % size) for i in range(size)]
+    out = jnp.zeros((*value.shape[:dim], size * extent, *value.shape[dim + 1 :]), value.dtype)
+    out = lax.dynamic_update_slice_in_dim(out, value, index * extent, axis=dim)
+    from_left = from_right = value
+    halfway = size // 2
+    for step in range(1, halfway + 1):
+        from_left = lax.ppermute(from_left, axis, right)
+        out = lax.dynamic_update_slice_in_dim(
+            out, from_left, (index - step) % size * extent, axis=dim
+        )
+        if step < size - halfway:
+            from_right = lax.ppermute(from_right, axis, left)
+            out = lax.dynamic_update_slice_in_dim(
+                out, from_right, (index + step) % size * extent, axis=dim
+            )
+    return out
 
 
 def halved(operand):
@@ -104,7 +125,7 @@
     whole = ("dp", "seq")
 
     def gather_rows(local):
-        full = lax.all_gather(local.reshape(slot_count, block_size, -1), "seq", axis=1, tiled=True)
+        full = collect(local.reshape(slot_count, block_size, -1), "seq", 1)
         return full.reshape(all_rows, -1)
 
     def scatter_rows(partial):

time: 883 us -> 830 us (0.940)
  waiting for transfers between devices: 723 us -> 662 us
  local copies, waits for them, and re-layouts: 33.8 us -> 45.2 us
  starting transfers between devices: 11.4 us -> 20.4 us
    all_gather x3 -> x0, waiting for transfers between devices: 48.7 us -> none  [gather_rows(): lax.all_gather(local.reshape(slot_count, block_size, -1), 'seq', axis=1,...]
    ppermute x0 -> x9, waiting for transfers between devices: none -> 14.1 us  [the longest x6 10.8 us: collect(): from_left = lax.ppermute(from_left, axis, right)]
    all_gather x1, waiting for transfers between devices: 29.5 us -> 16.2 us  [body(): up_part = lax.all_gather(moved_up, 'dp', axis=0, tiled=True)]
    all_to_all x2 -> x1, blocking collectives: 17.9 us -> 9.5 us  [spread_columns(): moved = lax.all_to_all(parts, 'seq', 2, 0, tiled=True)]
    unnamed x16 -> x13, waiting for transfers between devices: 123 us -> 123 us
  transfers between devices with their start and end apart: 18 -> 25, of which waited for: 18 -> 20; matrix products, arithmetic and copies ran while one was open for 7% -> 8% of each run, Pallas kernels for 0% -> 0%
where the time goes in v1:
time: 830 us; the launch traced here: 828 us
  waiting for transfers between devices  662 us (80%)
  local copies, waits for them, and re-layouts  45.2 us (5%)
  matrix products  38.4 us (5%)
  other arithmetic  28.6 us (3%)
  starting transfers between devices  20.4 us (2%)
  blocking collectives  18.6 us (2%)
  between operations  15.4 us (2%)
    reduce_scatter x1, waiting for transfers between devices, body(): lax.psum_scatter(outer(attended, middle_half), whole, scatter_dimension=0...  124 us
    unnamed x13, waiting for transfers between devices  123 us
    reduce_scatter x1, waiting for transfers between devices, body(): lax.psum_scatter(outer(active, cot_all), 'dp', scatter_dimension=0, tiled...  66.8 us
    reduce_scatter x3, waiting for transfers between devices, scatter_rows(): lax.psum_scatter(halved(partial).reshape(slot_count, length, -1), 'seq',...  63.5 us
    reduce_scatter x1, waiting for transfers between devices, body(): lax.psum_scatter(outer(lifted_two, upper_half), 'dp', scatter_dimension=0...  62.7 us
    reduce_scatter x1, waiting for transfers between devices, body(): lax.psum_scatter(outer(lifted_one, packed_grad), 'dp', scatter_dimension=...  60.6 us
    all_gather x1, waiting for transfers between devices, body(): down_part = lax.all_gather(halved(shrink), 'dp', axis=0, tiled=True)  48.2 us
    all_gather x1, waiting for transfers between devices, body(): lax.all_gather(jnp.concatenate([halved(outward), small_block], axis=0), w...  45.6 us
  transfers between devices with their start and end apart: 25, of which 20 were waited for; matrix products, arithmetic and copies ran while one was open for 8% of the time, Pallas kernels for 0%

profile of v1, /device:TPU:0, one launch (start us, length us, event | category | flops | bytes accessed | tf_op | source)
XLA Modules:
  0.0 828.2 jit_solution(13371358602193558532)
XLA Ops:
  12.5 9.5 %all_to_all.78 = bf16[32,3,4,256]{3,0,1,2:T(8,128)(2,1)S(1)} all-to-all(bf16[32,3,4,256]{3,0,1,2:T(8,128)(2,1)S(1)} %copy.236), channel_id=1, replica_groups=mesh['dp'=8,'seq'=4] {'seq'}, dimensions={2} | all-to-all | bytes 393216 | tf_op jit(solution)/shard_map/all_to_all | solution.py:82
  23.8 3.4 all-to-all-start.2
  27.9 45.6 %all-gather.5.cloned.1.call-done = bf16[1536,1024]{1,0:T(8,128)(2,1)} async-done(((bf16[48,1024]{1,0:T(8,128)(2,1)}), bf16[1536,1024]{1,0:T(8,128)(2,1)}) %all-gather.5.cloned.1.call-update) | async-done | bytes 3145744 | tf_op jit(solution)/shard_map/all_gather | solution.py:149
  77.2 1.6 collective-permute-start.1
  81.1 2.4 collective-permute-done
  85.5 5.5 collective-permute-done.2
  91.1 28.1 %all-gather.7.cloned.1.call-done = bf16[1024,768]{1,0:T(8,128)(2,1)} async-done(((bf16[128,768]{1,0:T(8,128)(2,1)}), bf16[1024,768]{1,0:T(8,128)(2,1)}) %all-gather.7.cloned.1.call-update) | async-done | bytes 1572880 | tf_op jit(solution)/shard_map/all_gather | solution.py:164
  119.1 2.7 fusion.89
  125.1 3.4 all-to-all-start.1
  128.6 1.7 collective-permute-start.7
  130.3 1.7 constant_dynamic-update-slice_fusion.7
  131.9 3.3 slice.165
  135.7 2.2 fusion.87
  139.0 1.7 constant_dynamic-update-slice_fusion.6
  140.6 1.7 constant_dynamic-update-slice_fusion.5
  146.8 2.5 collective-permute-done.4
  150.0 2.4 collective-permute-done.5
  153.1 16.2 %all-gather.9.cloned.1.call-done = bf16[1024,1024]{1,0:T(8,128)(2,1)} async-done(((bf16[128,1024]{1,0:T(8,128)(2,1)}), bf16[1024,1024]{1,0:T(8,128)(2,1)}) %all-gather.9.cloned.1.call-update) | async-done | bytes 2097168 | tf_op jit(solution)/shard_map/all_gather | solution.py:165
  169.3 3.2 fusion.90
  173.9 3.1 convolution_convert_fusion
  177.3 66.8 %reduce-scatter.23.cloned.1.call-done = bf16[128,1024]{1,0:T(8,128)(2,1)} async-done(((bf16[1024,1024]{1,0:T(8,128)(2,1)}), bf16[128,1024]{1,0:T(8,128)(2,1)}) %reduce-scatter.23.cloned.1.call-update) | async-done | bytes 262160 | tf_op jit(solution)/shard_map/reduce_scatter | solution.py:236
  244.0 2.1 fusion.55
  246.2 1.5 fusion.59
  247.7 48.2 %all-gather.11.cloned.1.call-done = bf16[1024,1024]{1,0:T(8,128)(2,1)} async-done(((bf16[128,1024]{1,0:T(8,128)(2,1)}), bf16[1024,1024]{1,0:T(8,128)(2,1)}) %all-gather.11.cloned.1.call-update) | async-done | bytes 2097168 | tf_op jit(solution)/shard_map/all_gather | solution.py:166
  295.9 5.1 fusion.88
  301.0 2.3 convolution_convert_fusion.5
  303.4 4.7 convolution_convert_fusion.6
  308.2 18.6 %reduce-scatter.13.cloned.1.call-done = bf16[2,64,1024]{2,1,0:T(8,128)(2,1)} async-done(((bf16[2,256,1024]{2,1,0:T(8,128)(2,1)}), bf16[2,64,1024]{2,1,0:T(8,128)(2,1)}) %reduce-scatter.13.cloned.1.call-update) | async-done | bytes 262160 | tf_op jit(solution)/shard_map/reduce_scatter | solution.py:132
  329.3 24.9 %reduce-scatter.11.cloned.1.call-done = bf16[2,64,1024]{2,1,0:T(8,128)(2,1)} async-done(((bf16[2,256,1024]{2,1,0:T(8,128)(2,1)}), bf16[2,64,1024]{2,1,0:T(8,128)(2,1)}) %reduce-scatter.11.cloned.1.call-update) | async-done | bytes 262160 | tf_op jit(solution)/shard_map/reduce_scatter | solution.py:132
  354.2 2.4 fusion.81
  358.5 1.5 reshape.573
  360.0 9.1 %all_to_all.79 = bf16[4,2,16384]{2,1,0:T(2,128)(2,1)} all-to-all(bf16[4,2,16384]{2,1,0:T(2,128)(2,1)S(1)} %reshape.573), channel_id=1, replica_groups=mesh['dp'=8,'seq'=4] {'seq'}, dimensions={0} | all-to-all | bytes 524288 | tf_op jit(solution)/shard_map/all_to_all | solution.py:256
  369.0 2.1 reshape.574
  371.2 2.3 copy.345
  378.9 2.0 convolution_convert_fusion.4
  381.0 3.8 convolution_convert_fusion.1
  385.9 20.0 %reduce-scatter.15.cloned.1.call-done = bf16[2,64,1024]{2,1,0:T(8,128)(2,1)} async-done(((bf16[2,256,1024]{2,1,0:T(8,128)(2,1)}), bf16[2,64,1024]{2,1,0:T(8,128)(2,1)}) %reduce-scatter.15.cloned.1.call-update) | async-done | bytes 262160 | tf_op jit(solution)/shard_map/reduce_scatter | solution.py:132
  408.4 3.4 convolution_convert_fusion.3
  413.2 2.1 convolution_convert_fusion.2
  415.3 62.7 %reduce-scatter.21.cloned.1.call-done = bf16[128,1024]{1,0:T(8,128)(2,1)} async-done(((bf16[1024,1024]{1,0:T(8,128)(2,1)}), bf16[128,1024]{1,0:T(8,128)(2,1)}) %reduce-scatter.21.cloned.1.call-update) | async-done | bytes 262160 | tf_op jit(solution)/shard_map/reduce_scatter | solution.py:240
  477.9 1.7 copy.304
  479.6 3.4 all-to-all-start.5
  484.6 4.5 all-to-all-done.5
  492.4 122.4 %reduce-scatter.25.cloned.1.call-done = f32[32,12]{1,0:T(8,128)} async-done(((f32[1024,12]{1,0:T(8,128)}), f32[32,12]{1,0:T(8,128)}) %reduce-scatter.25.cloned.1.call-update) | async-done | bytes 1552
  619.3 60.6 %reduce-scatter.17.cloned.1.call-done = bf16[128,768]{1,0:T(8,128)(2,1)} async-done(((bf16[1024,768]{1,0:T(8,128)(2,1)}), bf16[128,768]{1,0:T(8,128)(2,1)}) %reduce-scatter.17.cloned.1.call-update) | async-done | bytes 196624 | tf_op jit(solution)/shard_map/reduce_scatter | solution.py:290
  681.9 3.5 all-to-all-start.4
  687.2 4.9 all-to-all-done.4
  695.1 123.8 %reduce-scatter.19.cloned.1.call-done = bf16[32,1024]{1,0:T(8,128)(2,1)} async-done(((bf16[1024,1024]{1,0:T(8,128)(2,1)}), bf16[32,1024]{1,0:T(8,128)(2,1)}) %reduce-scatter.19.cloned.1.call-update) | async-done | bytes 65552 | tf_op jit(solution)/shard_map/reduce_scatter | solution.py:260
  (308 shorter events, 60.8 us)
Async XLA Ops:
  7.2 15.7 %copy-start.16 = (f32[32,4096]{1,0:T(8,128)S(1)}, f32[32,4096]{1,0:T(8,128)}, u32[]{:S(2)}) copy-start(f32[32,4096]{1,0:T(8,128)} %param.23) | copy-start | bytes 1572868
  7.2 66.2 %all-gather.5.cloned.1.call-start = ((), (), s32[]{:S(2)}) async-start(), calls=%async_computation.14 | async-start | bytes 3244032 | tf_op jit(solution)/shard_map/all_gather | solution.py:149
  11.2 107.9 %all-gather.7.cloned.1.call-start = ((), (), s32[]{:S(2)}) async-start(), calls=%async_computation.15 | async-start | bytes 1769472 | tf_op jit(solution)/shard_map/all_gather | solution.py:164
  12.4 14.9 %copy-start.52 = (s32[8]{0:T(128)S(1)}, s32[8]{0:T(128)}, u32[]{:S(2)}) copy-start(s32[8]{0:T(128)} %param.19) | copy-start | bytes 100
  12.4 15.1 %copy-start.1 = (f32[2,64,1024]{2,1,0:T(8,128)S(1)}, f32[2,64,1024]{2,1,0:T(8,128)}, u32[]{:S(2)}) copy-start(f32[2,64,1024]{2,1,0:T(8,128)} %param.17) | copy-start | bytes 1572868
  23.8 59.7 %all-to-all-start.2 = ((bf16[32,8,4,128]{3,1,0,2:T(8,128)(2,1)}), bf16[32,8,4,128]{3,1,0,2:T(8,128)(2,1)S(1)}, u32[]{:S(2)}, u32[]{:S(2)}) async-start(bf16[32,8,4,128]{3,1,0,2:T(8,128)(2,1)} %copy.248), calls=%async_computation.2 | async-start | bytes 524288 | tf_op jit(solution)/shard_map/all_to_all | solution.py:82
  27.2 142.1 %all-gather.9.cloned.1.call-start = ((), (), s32[]{:S(2)}) async-start(), calls=%async_computation.16 | async-start | bytes 2359296 | tf_op jit(solution)/shard_map/all_gather | solution.py:165
  27.5 49.5 %copy-start.46 = (f32[2]{0:T(128)}, f32[2]{0:T(128)S(1)}, u32[]{:S(2)}) copy-start(f32[2]{0:T(128)S(1)} %convert_element_type.217) | copy-start | bytes 28
  76.7 6.7 collective-permute-start
  77.2 8.3 collective-permute-start.1
  80.6 49.6 %collective-permute-start.6 = (bf16[2,64,1024]{2,1,0:T(8,128)(2,1)}, bf16[2,64,1024]{2,1,0:T(8,128)(2,1)}, u32[]{:S(2)}, u32[]{:S(2)}) collective-permute-start(bf16[2,64,1024]{2,1,0:T(8,128)(2,1)} %get-tuple-element.209), channel_id=1, source_target_pairs={{0,1},{1,2},{2,3},{3,0},{4,5},{5,6},{6,7},{7,4},{8,9},{9,10},{10,1... | collective-permute-start | bytes 786440 | tf_op jit(solution)/shard_map/ppermute | solution.py:30
  83.4 7.6 collective-permute-start.2
  91.1 28.1 %copy-start.25 = (bf16[2,256,1024]{2,1,0:T(8,128)(2,1)}, bf16[2,256,1024]{2,1,0:T(8,128)(2,1)S(1)}, u32[]{:S(2)}) copy-start(bf16[2,256,1024]{2,1,0:T(8,128)(2,1)S(1)} %constant_dynamic-update-slice_fusion.13) | copy-start | bytes 3145732
  124.2 11.0 %copy-start.8 = (bf16[2,4,256,64]{2,3,1,0:T(8,128)(2,1)}, bf16[2,4,256,64]{2,3,1,0:T(8,128)(2,1)S(1)}, u32[]{:S(2)}) copy-start(bf16[2,4,256,64]{2,3,1,0:T(8,128)(2,1)S(1)} %convolution_convert_fusion.7) | copy-start | bytes 786436
  125.1 10.3 %all-to-all-start.1 = ((bf16[2,256,256]{2,0,1:T(2,128)(2,1)}), bf16[2,256,256]{2,0,1:T(2,128)(2,1)S(1)}, u32[]{:S(2)}, u32[]{:S(2)}) async-start(bf16[2,256,256]{2,0,1:T(2,128)(2,1)} %copy.245), calls=%async_computation.1 | async-start | bytes 524288 | tf_op jit(solution)/shard_map/all_to_all | solution.py:202
  128.5 115.5 %reduce-scatter.23.cloned.1.call-start = ((), (), s32[]{:S(2)}) async-start(), calls=%async_computation.24 | async-start | bytes 2359296 | tf_op jit(solution)/shard_map/reduce_scatter | solution.py:236
  128.6 10.4 %collective-permute-start.7 = (bf16[2,64,1024]{2,1,0:T(8,128)(2,1)}, bf16[2,64,1024]{2,1,0:T(8,128)(2,1)}, u32[]{:S(2)}, u32[]{:S(2)}) collective-permute-start(bf16[2,64,1024]{2,1,0:T(8,128)(2,1)} %get-tuple-element.209), channel_id=1, source_target_pairs={{0,3},{1,0},{2,1},{3,2},{4,7},{5,4},{6,5},{7,6},{8,11},{9,8},{10,9... | collective-permute-start | bytes 786440 | tf_op jit(solution)/shard_map/ppermute | solution.py:35
  130.3 10.4 %collective-permute-start.8 = (bf16[2,64,1024]{2,1,0:T(8,128)(2,1)}, bf16[2,64,1024]{2,1,0:T(8,128)(2,1)}, u32[]{:S(2)}, u32[]{:S(2)}) collective-permute-start(bf16[2,64,1024]{2,1,0:T(8,128)(2,1)} %collective-permute-done.6), channel_id=1, source_target_pairs={{0,1},{1,2},{2,3},{3,0},{4,5},{5,6},{6,7},{7,4},{8,9},{9,10},{10,1... | collective-permute-start | bytes 786440 | tf_op jit(solution)/shard_map/ppermute | solution.py:30
  138.4 5.9 collective-permute-start.3
  142.3 7.0 collective-permute-start.4
  144.3 8.1 collective-permute-start.5
  177.0 118.9 %all-gather.11.cloned.1.call-start = ((), (), s32[]{:S(2)}) async-start(), calls=%async_computation.17 | async-start | bytes 2359296 | tf_op jit(solution)/shard_map/all_gather | solution.py:166
  247.7 79.2 %reduce-scatter.13.cloned.1.call-start = ((), (), s32[]{:S(2)}) async-start(), calls=%async_computation.19 | async-start | bytes 1310720 | tf_op jit(solution)/shard_map/reduce_scatter | solution.py:132
  295.9 5.1 copy-start.50
  303.3 50.8 %reduce-scatter.11.cloned.1.call-start = ((), (), s32[]{:S(2)}) async-start(), calls=%async_computation.18 | async-start | bytes 1310720 | tf_op jit(solution)/shard_map/reduce_scatter | solution.py:132
  308.1 97.8 %reduce-scatter.15.cloned.1.call-start = ((), (), s32[]{:S(2)}) async-start(), calls=%async_computation.20 | async-start | bytes 1310720 | tf_op jit(solution)/shard_map/reduce_scatter | solution.py:132
  358.5 16.4 %copy-start.9 = (bf16[2,4,256,64]{2,3,1,0:T(8,128)(2,1)S(1)}, bf16[2,4,256,64]{2,3,1,0:T(8,128)(2,1)}, u32[]{:S(2)}) copy-start(bf16[2,4,256,64]{2,3,1,0:T(8,128)(2,1)} %copy-done.8) | copy-start | bytes 786436
  381.0 97.0 %reduce-scatter.21.cloned.1.call-start = ((), (), s32[]{:S(2)}) async-start(), calls=%async_computation.23 | async-start | bytes 2359296 | tf_op jit(solution)/shard_map/reduce_scatter | solution.py:240
  384.9 23.5 %copy-start.26 = (bf16[2,256,1024]{2,1,0:T(8,128)(2,1)S(1)}, bf16[2,256,1024]{2,1,0:T(8,128)(2,1)}, u32[]{:S(2)}) copy-start(bf16[2,256,1024]{2,1,0:T(8,128)(2,1)} %copy-done.25) | copy-start | bytes 3145732
  384.9 230.0 %reduce-scatter.25.cloned.1.call-start = ((), (), s32[]{:S(2)}) async-start(), calls=%async_computation.25 | async-start | bytes 540672
  408.4 271.6 %reduce-scatter.17.cloned.1.call-start = ((), (), s32[]{:S(2)}) async-start(), calls=%async_computation.21 | async-start | bytes 1769472 | tf_op jit(solution)/shard_map/reduce_scatter | solution.py:290
  411.9 407.1 %reduce-scatter.19.cloned.1.call-start = ((), (), s32[]{:S(2)}) async-start(), calls=%async_computation.22 | async-start | bytes 2162688 | tf_op jit(solution)/shard_map/reduce_scatter | solution.py:260
  415.2 68.0 %copy-start.29 = (bf16[2,64,1024]{2,1,0:T(8,128)(2,1)S(1)}, bf16[2,64,1024]{2,1,0:T(8,128)(2,1)}, u32[]{:S(2)}) copy-start(bf16[2,64,1024]{2,1,0:T(8,128)(2,1)} %reduce-scatter.15.cloned.1.call-done) | copy-start | bytes 786436
  415.2 68.2 %copy-start.21 = (f32[128,1024]{1,0:T(8,128)S(1)}, f32[128,1024]{1,0:T(8,128)}, u32[]{:S(2)}) copy-start(f32[128,1024]{1,0:T(8,128)} %get-tuple-element.225) | copy-start | bytes 1572868
  415.2 68.2 %copy-start.47 = (f32[2]{0:T(128)S(1)}, f32[2]{0:T(128)}, u32[]{:S(2)}) copy-start(f32[2]{0:T(128)} %copy-done.46) | copy-start | bytes 28
  479.6 9.5 %all-to-all-start.5 = ((bf16[128,8,1,128]{3,1,2,0:T(8,128)(2,1)}), bf16[128,8,1,128]{3,1,2,0:T(8,128)(2,1)S(1)}, u32[]{:S(2)}, u32[]{:S(2)}) async-start(bf16[128,8,1,128]{3,1,2,0:T(8,128)(2,1)} %bitcast.49), calls=%async_computation.11 | async-start | bytes 524288 | tf_op jit(solution)/shard_map/all_to_all | solution.py:89
  484.6 5.3 copy-start.5
  490.1 127.4 %copy-start.40 = (f32[5,32]{1,0:T(8,128)S(1)}, f32[5,32]{1,0:T(8,128)}, u32[]{:S(2)}) copy-start(f32[5,32]{1,0:T(8,128)} %param.22) | copy-start | bytes 1924
  490.2 128.0 %copy-start.44 = (f32[2,128]{1,0:T(2,128)S(1)}, f32[2,128]{1,0:T(2,128)}, u32[]{:S(2)}) copy-start(f32[2,128]{1,0:T(2,128)} %param.33) | copy-start | bytes 3076
  490.2 128.0 %copy-start.49 = (f32[128]{0:T(128)S(1)}, f32[128]{0:T(128)}, u32[]{:S(2)}) copy-start(f32[128]{0:T(128)} %param.26) | copy-start | bytes 1540
  490.2 128.5 %copy-start.42 = (f32[3,32]{1,0:T(4,128)S(1)}, f32[3,32]{1,0:T(4,128)}, u32[]{:S(2)}) copy-start(f32[3,32]{1,0:T(4,128)} %param.25) | copy-start | bytes 1156
  615.8 77.0 %copy-start.48 = (f32[128]{0:T(128)}, f32[128]{0:T(128)S(1)}, u32[]{:S(2)}) copy-start(f32[128]{0:T(128)S(1)} %reshape.514) | copy-start | bytes 1540
  616.7 76.3 %copy-start.39 = (f32[32,5]{0,1:T(8,128)}, f32[32,5]{0,1:T(8,128)S(1)}, u32[]{:S(2)}) copy-start(f32[32,5]{0,1:T(8,128)S(1)} %copy.292) | copy-start | bytes 1924
  617.5 75.4 %copy-start.41 = (f32[32,3]{0,1:T(4,128)}, f32[32,3]{0,1:T(4,128)S(1)}, u32[]{:S(2)}) copy-start(f32[32,3]{0,1:T(4,128)S(1)} %copy.293) | copy-start | bytes 1156
  681.9 11.0 %copy-start.6 = (f32[2,32,3072]{2,1,0:T(8,128)S(1)}, f32[2,32,3072]{2,1,0:T(8,128)}, u32[]{:S(2)}) copy-start(f32[2,32,3072]{2,1,0:T(8,128)} %param.27) | copy-start | bytes 2359300
  681.9 10.2 %all-to-all-start.4 = ((bf16[128,3,1,256]{3,1,2,0:T(4,128)(2,1)}), bf16[128,3,1,256]{3,1,2,0:T(4,128)(2,1)S(1)}, u32[]{:S(2)}, u32[]{:S(2)}) async-start(bf16[128,3,1,256]{3,1,2,0:T(4,128)(2,1)} %copy.263), calls=%async_computation.8 | async-start | bytes 524288 | tf_op jit(solution)/shard_map/all_to_all | solution.py:89
  693.1 125.8 %copy-start.30 = (f32[2,32,1024]{2,1,0:T(8,128)S(1)}, f32[2,32,1024]{2,1,0:T(8,128)}, u32[]{:S(2)}) copy-start(f32[2,32,1024]{2,1,0:T(8,128)} %param.28) | copy-start | bytes 786436
  693.1 126.7 %copy-start.33 = (f32[32,1024]{1,0:T(8,128)S(1)}, f32[32,1024]{1,0:T(8,128)}, u32[]{:S(2)}) copy-start(f32[32,1024]{1,0:T(8,128)} %param.21) | copy-start | bytes 393220
  (33 other events, 69.6 us)
Sparse Core Ops, SparseCore 0:
  11.5 61.8 all-gather.4
  76.2 42.8 all-gather.6
  121.8 47.4 all-gather.8
  177.1 66.8 reduce-scatter.22
  247.8 48.1 all-gather.10
  303.5 23.3 reduce-scatter.12
  329.4 24.7 reduce-scatter.10
  381.1 24.8 reduce-scatter.14
  409.5 68.4 reduce-scatter.20
  480.0 134.7 reduce-scatter.24
  618.3 61.6 reduce-scatter.16
  682.1 136.8 reduce-scatter.18
